TPU v7x, 256 devices: a whole 4x4x8 slice. The times are simulated.
256 devices in a mesh: tm: 16 (over y, x), space: 2 (over core), head: 8 (over z).
Axes of the slice: x: 4, y: 4, z: 8, core: 2. Of those that a mesh axis runs over, the one named last changes fastest.
Arguments:
- query: bfloat16 [16, 8, 80, 5120], P('tm', 'space', None, 'head'), may hold values from -5 to 5
- key: bfloat16 [16, 8, 80, 5120], P('tm', 'space', None, 'head'), may hold values from -5 to 5
- value: bfloat16 [16, 8, 80, 5120], P('tm', 'space', None, 'head'), may hold values from -6 to 6
- window: int32 [16, 16], replicated, may hold values from -1 to 4, as said below
- out_weight: bfloat16 [5120, 5120], P('head'), may hold values from -0.078125 to 0.078125
Outputs:
- projected: bfloat16 [16, 8, 80, 5120], P('tm', 'space', None, 'head')
Inputs may be any that keep to these rules, and one draw needn't show every extreme that they name: window[f, f] = 4 for every frame f.
All inputs are finite; a program needn't handle non-finite values.
Results may differ from a plain program's by a relative error of at most 0.023.
Values may be sent and summed in bfloat16 or wider, within the bound.
A program may use at most 128 MiB of HBM per device.

v0:
```python
import math

import jax
import jax.numpy as jnp
from jax import lax
from jax.sharding import PartitionSpec as P

HD = 128
HALO = 4


NEG_FILL = -1e30


def padded_2(x, sides, width):
    for axis, dim in sides:
        size, length = (lax.axis_size(axis), x.shape[dim])
        up = [(i, (i + 1) % size) for i in range(size - 1)]
        down = [(j, i) for i, j in up]
        last = lax.slice_in_dim(x, length - width, length, axis=dim)
        first = lax.slice_in_dim(x, 0, width, axis=dim)
        before = lax.ppermute(last, axis, up)
        after = lax.ppermute(first, axis, down)
        x = jnp.concatenate([before, x, after], axis=dim)
    return x


def frame_mask(widths, query_rows, key_rows, total_rows, width):
    count = widths.shape[0]
    distance = jnp.abs(query_rows[:, None] - key_rows[None, :])
    inside_grid = (key_rows >= 0) & (key_rows < total_rows)
    inside = (
        (widths[:, None, None] >= 0)
        & (distance[None] <= widths[:, None, None])
        & inside_grid[None, None, :]
    )
    span_rows = key_rows.shape[0]
    full = jnp.broadcast_to(
        inside[:, :, None, :, None], (count, query_rows.shape[0], width, span_rows, width)
    )
    return full.reshape(count * query_rows.shape[0] * width, span_rows * width)


def absorb(state, queries, keys, values, mask):
    run_max, run_sum, run_acc = state
    scale = 1.0 / math.sqrt(HD)
    scores = jnp.einsum("qhd,khd->hqk", queries, keys, preferred_element_type=jnp.float32) * scale
    new_max = jnp.maximum(run_max, jnp.max(jnp.where(mask[None], scores, NEG_FILL), axis=-1))
    weights = jnp.where(mask[None], jnp.exp(scores - new_max[..., None]), 0.0)
    factor = jnp.exp(run_max - new_max)
    new_sum = run_sum * factor + jnp.sum(weights, axis=-1)
    new_acc = run_acc * factor[..., None] + jnp.einsum(
        "hqk,khd->hqd", weights.astype(jnp.bfloat16), values, preferred_element_type=jnp.float32
    )
    return (new_max, new_sum, new_acc)


def absorb_frame(state, queries, widths, kv_frame, query_rows, key_rows, total_rows):
    span_rows, width, feats = (kv_frame.shape[1], kv_frame.shape[2], kv_frame.shape[3])
    heads_dev = feats // HD
    keys = kv_frame[0].reshape(span_rows * width, heads_dev, HD)
    values = kv_frame[1].reshape(span_rows * width, heads_dev, HD)
    mask = frame_mask(widths, query_rows, key_rows, total_rows, width)
    return absorb(state, queries, keys, values, mask)


def empty_state(heads_dev, count):
    return (
        jnp.full((heads_dev, count), NEG_FILL, jnp.float32),
        jnp.zeros((heads_dev, count), jnp.float32),
        jnp.zeros((heads_dev, count, HD), jnp.float32),
    )


def body(query, key, value, window, out_weight):
    frames_dev, rows_dev, width, feats = query.shape
    heads_dev = feats // HD
    qcount = frames_dev * rows_dev * width
    total_rows = rows_dev * lax.axis_size("space")
    first_row = lax.axis_index("space") * rows_dev
    first_frame = lax.axis_index("tm") * frames_dev
    query_rows = first_row + jnp.arange(rows_dev, dtype=jnp.int32)
    stacked = jnp.stack([key, value])
    padded = padded_2(stacked, (("space", 2),), HALO)
    key_rows = first_row - HALO + jnp.arange(rows_dev + 2 * HALO, dtype=jnp.int32)
    my_windows = lax.dynamic_slice_in_dim(window, first_frame, frames_dev, 0)
    queries = query.reshape(qcount, heads_dev, HD)
    piece = lax.all_gather(padded, "tm", axis=1, tiled=True)

    def one_frame(carry, offset):
        kv_frame = lax.dynamic_index_in_dim(piece, offset, 1, False)
        widths = lax.dynamic_index_in_dim(my_windows, offset, 1, False)
        return (
            absorb_frame(carry, queries, widths, kv_frame, query_rows, key_rows, total_rows),
            None,
        )

    result, unused = lax.scan(
        one_frame, empty_state(heads_dev, qcount), jnp.arange(piece.shape[1], dtype=jnp.int32)
    )
    run_max, run_sum, run_acc = result
    attended = (
        (run_acc / run_sum[..., None])
        .transpose(1, 0, 2)
        .reshape(qcount, feats)
        .astype(jnp.bfloat16)
    )
    share_rows = out_weight.shape[1] // lax.axis_size("head")
    mixed = lax.psum_scatter(
        lax.dot_general(
            out_weight, attended, (((0,), (1,)), ((), ())), preferred_element_type=jnp.float32
        ).astype(jnp.bfloat16),
        "head",
        scatter_dimension=0,
        tiled=True,
    ).astype(jnp.float32)
    return mixed.T.reshape(frames_dev, rows_dev, width, share_rows).astype(jnp.bfloat16)


def solution(mesh):
    placed = (
        P("tm", "space", None, "head"),
        P("tm", "space", None, "head"),
        P("tm", "space", None, "head"),
        P(),
        P("head", None),
    )
    return jax.shard_map(
        body, mesh=mesh, in_specs=placed, out_specs=P("tm", "space", None, "head"), check_vma=False
    )
```

profile of v0, /device:TPU:8, one launch (start us, length us, event | category | flops | bytes accessed | tf_op | source)
XLA Modules:
  0.0 809.1 jit_solution(69779024183798448)
XLA Ops:
  18.7 232.5 %all-gather.2.cloned.1.call-done = bf16[2,16,12,80,640]{4,3,2,1,0:T(8,128)(2,1)} async-done(((bf16[2,1,12,80,640]{4,3,2,1,0:T(8,128)(2,1)}), bf16[2,16,12,80,640]{4,3,2,1,0:T(8,128)(2,1)}) %all-gather.2.cloned.1.call-update) | async-done | bytes 39321616 | tf_op jit(solution)/shard_map/all_gather | solution.py:88
  251.2 484.5 %while.15 = (s32[]{:T(128)}, f32[5,320]{1,0:T(8,128)S(1)}, f32[5,320]{1,0:T(8,128)}, f32[5,320,128]{2,1,0:T(8,128)}, s32[16]{0:T(128)S(1)}, /*index=5*/s32[1,16]...) while((s32[]{:T(128)}, f32[5,320]{1,0:T(8,128)S(1)}, ...), condition=%wide.region_3.4_spmd.clone, body=%wide.region_0.3_spmd.clone.sunk | while | flops 803950720 | bytes 35329148 | solution.py:98
  262.4 5.7 fusion.43
  268.2 4.9 fusion.44
  275.1 5.5 fusion.46
  291.9 5.7 fusion.43
  297.7 4.9 fusion.44
  305.3 5.7 fusion.46
  322.3 5.7 fusion.43
  335.6 5.7 fusion.46
  352.6 5.7 fusion.43
  358.3 4.9 fusion.44
  366.0 5.7 fusion.46
  382.9 5.7 fusion.43
  388.7 4.9 fusion.44
  396.3 5.7 fusion.46
  413.3 5.7 fusion.43
  419.0 4.9 fusion.44
  426.6 5.7 fusion.46
  443.6 5.7 fusion.43
  449.3 4.9 fusion.44
  457.0 5.7 fusion.46
  473.9 5.7 fusion.43
  487.3 5.7 fusion.46
  504.2 5.7 fusion.43
  510.0 4.9 fusion.44
  517.6 5.7 fusion.46
  534.6 5.7 fusion.43
  540.3 4.9 fusion.44
  548.0 5.7 fusion.46
  564.9 5.7 fusion.43
  570.6 4.9 fusion.44
  578.3 5.7 fusion.46
  595.2 5.7 fusion.43
  601.0 4.9 fusion.44
  608.6 5.7 fusion.46
  625.6 5.7 fusion.43
  631.3 4.9 fusion.44
  639.0 5.7 fusion.46
  655.9 5.7 fusion.43
  661.6 4.9 fusion.44
  669.3 5.7 fusion.46
  686.2 5.7 fusion.43
  699.6 5.7 fusion.46
  716.6 5.7 fusion.43
  730.0 5.7 fusion.46
  738.1 5.8 fusion.23
  747.5 52.8 %reduce-scatter.4.cloned.1.call-done = bf16[640,320]{1,0:T(8,128)(2,1)} async-done(((bf16[5120,320]{1,0:T(8,128)(2,1)}), bf16[640,320]{1,0:T(8,128)(2,1)}) %reduce-scatter.4.cloned.1.call-update) | async-done | bytes 409616
  (351 shorter events, 233.1 us)
Async XLA Ops:
  6.5 11.6 %copy-start = (s32[16,16]{1,0:T(8,128)S(1)}, s32[16,16]{1,0:T(8,128)}, u32[]{:S(2)}) copy-start(s32[16,16]{1,0:T(8,128)} %param.10) | copy-start | bytes 3076
  6.5 10.3 %copy-start.2 = (bf16[1,4,80,640]{3,2,1,0:T(8,128)(2,1)S(1)}, bf16[1,4,80,640]{3,2,1,0:T(8,128)(2,1)}, u32[]{:S(2)}) copy-start(bf16[1,4,80,640]{3,2,1,0:T(8,128)(2,1)} %param.7) | copy-start | bytes 1228804
  6.5 244.6 %all-gather.2.cloned.1.call-start = ((), (), s32[]{:S(2)}) async-start(), calls=%async_computation.1 | async-start | bytes 41779200 | tf_op jit(solution)/shard_map/all_gather | solution.py:88
  7.8 3.7 collective-permute-start
  9.6 4.2 collective-permute-start.1
  16.7 783.6 %reduce-scatter.4.cloned.1.call-start = ((), (), s32[]{:S(2)}) async-start(), calls=%async_computation.2 | async-start | bytes 4423680
  251.2 3.7 copy-start.3
  275.1 5.5 copy-start.4
  280.6 3.7 copy-start.3
  305.3 5.7 copy-start.4
  311.0 3.7 copy-start.3
  335.6 5.7 copy-start.4
  341.3 3.7 copy-start.3
  366.0 5.7 copy-start.4
  371.6 3.7 copy-start.3
  396.3 5.7 copy-start.4
  402.0 3.7 copy-start.3
  426.6 5.7 copy-start.4
  432.3 3.7 copy-start.3
  457.0 5.7 copy-start.4
  462.6 3.7 copy-start.3
  487.3 5.7 copy-start.4
  493.0 3.7 copy-start.3
  517.6 5.7 copy-start.4
  523.3 3.7 copy-start.3
  548.0 5.7 copy-start.4
  553.6 3.7 copy-start.3
  578.3 5.7 copy-start.4
  584.0 3.7 copy-start.3
  608.6 5.7 copy-start.4
  614.3 3.7 copy-start.3
  639.0 5.7 copy-start.4
  644.6 3.7 copy-start.3
  669.3 5.7 copy-start.4
  675.0 3.7 copy-start.3
  699.6 5.7 copy-start.4
  705.3 3.7 copy-start.3
  730.0 5.7 copy-start.4
  738.1 64.2 %copy-start.1 = (s32[16,16]{1,0:T(8,128)S(1)}, s32[16,16]{1,0:T(8,128)}, u32[]{:S(2)}) copy-start(s32[16,16]{1,0:T(8,128)} %param.10) | copy-start | bytes 3076
Sparse Core Ops, SparseCore 0:
  16.8 234.2 all-gather.1
  747.6 52.6 reduce-scatter.3
where the time goes:
time: 813 us; the launch traced here: 809 us
  waiting for transfers between devices  288 us (35%)
  matrix products  188 us (23%)
  other arithmetic  145 us (18%)
  local copies, waits for them, and re-layouts  141 us (17%)
  loops' own time  30.9 us (4%)
  between operations  13.5 us (2%)
    all_gather x1, waiting for transfers between devices, body(): piece = lax.all_gather(padded, 'tm', axis=1, tiled=True)  232 us
    dot_general x16, matrix products, absorb(): jnp.einsum('qhd,khd->hqk', queries, keys, preferred_element_type=jnp.floa...  91.6 us
    dot_general x16, matrix products, absorb(): jnp.einsum('hqk,khd->hqd', weights.astype(jnp.bfloat16), values, preferre...  90.3 us
    reduce_sum x16, other arithmetic, absorb(): new_sum = run_sum * factor + jnp.sum(weights, axis=-1)  78.2 us
    unnamed x3, waiting for transfers between devices  52.8 us
    squeeze x16, local copies, waits for them, and re-layouts, absorb_frame(): keys = kv_frame[0].reshape(span_rows * width, heads_dev, HD)  42.2 us
    another operation x1, loops' own time, body(): lax.scan(one_frame, empty_state(heads_dev, qcount), jnp.arange(piece.shap...  30.9 us
    slice x16, local copies, waits for them, and re-layouts, absorb_frame(): values = kv_frame[1].reshape(span_rows * width, heads_dev, HD)  30 us
  transfers between devices with their start and end apart: 4, of which 4 were waited for; matrix products, arithmetic and copies ran while one was open for 0% of the time, Pallas kernels for 0%

commit v1 on v0

v1 whole, which is shorter than its diff:
```python
import functools
import math

import jax
import jax.numpy as jnp
from jax import lax
from jax.experimental import pallas as pl
from jax.experimental.pallas import tpu as pltpu
from jax.sharding import PartitionSpec as P

HD = 128
SIDE = 4
NEG_FILL = -1e30
MAX_START = -1e20
MESH = pl.DeviceIdType.MESH

GRAY = (0, 1, 3, 2)
MAIN_ORDER = (
    (0, 0), (0, 1), (-1, 0), (0, 2), (1, 0), (0, 3), (-1, 1), (1, 1),
    (-1, 2), (1, 2), (2, 0), (2, 1), (-1, 3), (1, 3), (2, 2), (2, 3),
)
LAST_ORDER = (
    (0, 0), (0, 1), (0, 2), (0, 3), (-1, 0), (1, 0), (-1, 1), (1, 1),
    (-1, 2), (1, 2), (2, 0), (2, 1), (-1, 3), (1, 3), (2, 2), (2, 3),
)
PLUS = (0, 2)
MINUS = (1, 3)
N_SENDS = 96


def pick(index, values):
    out = values[0]
    for position, value in enumerate(values[1:], 1):
        out = jnp.where(index == position, value, out)
    return out


def greet(partners):
    barrier = pltpu.get_barrier_semaphore()
    for partner in partners:
        pl.semaphore_signal(barrier, inc=1, device_id=partner, device_id_type=MESH)
    pl.semaphore_wait(barrier, len(partners))


def attend_kernel(
    window, q_ref, k_ref, v_ref, o_ref,
    kv_main, kv_last, q_main, far, s_even, s_odd, run_max, run_sum, run_acc,
    send_sem, main_sem, last_sem, main_pair_sem, last_pair_sem, q_sem, local_sem,
):
    scale = math.log2(math.e) / math.sqrt(HD)
    tm, core = lax.axis_index("tm"), lax.axis_index("space")
    y, x = tm // SIDE, tm % SIDE
    frame = {
        (dy, dx): ((y + dy) % SIDE) * SIDE + (x + dx) % SIDE for dy in range(4) for dx in range(4)
    }
    up, down, across_y = ({"tm": frame[(d, 0)]} for d in (1, 3, 2))
    right, left, across_x = ({"tm": frame[(0, d)]} for d in (1, 3, 2))
    pair = {"space": 1 - core}
    greet([up, down, across_y, right, left, across_x, pair])

    counts = {"piece": 0, "block": 0}
    block = 320
    tokens = k_ref.shape[0]

    def send(src, dst, recv_sem, device, kind="piece"):
        slot = counts["piece"] if kind == "piece" else N_SENDS - 1 - counts["block"]
        counts[kind] += 1
        pltpu.make_async_remote_copy(
            src_ref=src, dst_ref=dst, send_sem=send_sem.at[slot], recv_sem=recv_sem,
            device_id=device, device_id_type=MESH,
        ).start()

    def head_of(ref, head):
        return ref.at[:, pl.ds(pl.multiple_of(head * HD, HD), HD)]

    mine = frame[(0, 0)]
    local = [
        pltpu.make_async_copy(head_of(q_ref, x), q_main.at[x], local_sem.at[0]),
        pltpu.make_async_copy(head_of(k_ref, x), kv_main.at[mine, core, 0], local_sem.at[1]),
        pltpu.make_async_copy(head_of(v_ref, x), kv_main.at[mine, core, 1], local_sem.at[2]),
        pltpu.make_async_copy(head_of(k_ref, SIDE), kv_last.at[mine, core, 0], local_sem.at[3]),
        pltpu.make_async_copy(head_of(v_ref, SIDE), kv_last.at[mine, core, 1], local_sem.at[4]),
    ]
    for copy in local:
        copy.start()
    partners = ((1, right), (3, left), (2, across_x))
    for dx, device in partners:
        send(head_of(q_ref, (x + dx) % SIDE), q_main.at[x], q_sem.at[x], device, "block")
    for dx, device in partners:
        other = (x + dx) % SIDE
        send(head_of(k_ref, other), kv_main.at[mine, core, 0], main_sem.at[mine], device, "block")
        send(head_of(v_ref, other), kv_main.at[mine, core, 1], main_sem.at[mine], device, "block")
    for copy in local:
        copy.wait()

    def pass_main(f, device):
        send(kv_main.at[f, core], kv_main.at[f, core], main_sem.at[f], device)

    def pass_last(f, device):
        send(kv_last.at[f, core], kv_last.at[f, core], last_sem.at[f], device)

    def share(ref, f, sems):
        send(ref.at[f, core], ref.at[f, core], sems.at[f], pair)

    pass_last(mine, up)
    pass_last(mine, down)
    pass_last(mine, right)
    pass_last(mine, left)
    pass_main(mine, up)
    pass_main(mine, down)
    pass_last(mine, across_y)
    share(kv_main, mine, main_pair_sem)
    share(kv_last, mine, last_pair_sem)

    query_row = lax.broadcasted_iota(jnp.int32, (tokens, 2 * tokens), 0) // 80 + core * (tokens // 80)
    key_row = lax.broadcasted_iota(jnp.int32, (tokens, 2 * tokens), 1) // 80
    far[...] = jnp.abs(query_row - key_row)
    run_max[...] = jnp.full_like(run_max, MAX_START)
    run_sum[...] = jnp.zeros_like(run_sum)
    run_acc[...] = jnp.zeros_like(run_acc)

    def arrived(ref, f, sems):
        pltpu.make_async_remote_copy(
            src_ref=ref.at[f, core], dst_ref=ref.at[f, core], send_sem=send_sem.at[0], recv_sem=sems.at[f],
            device_id=pair, device_id_type=MESH,
        ).wait_recv()

    def arrived_pair(ref, f, sems):
        pltpu.make_async_remote_copy(
            src_ref=ref.at[f, 1 - core], dst_ref=ref.at[f, 1 - core], send_sem=send_sem.at[0],
            recv_sem=sems.at[f], device_id=pair, device_id_type=MESH,
        ).wait_recv()

    def main_frame(entry):
        across, along = entry
        return frame[(across % SIDE, GRAY[along])]

    def last_frame(entry):
        across, along = entry
        return frame[(GRAY[along], across % SIDE)]

    def take_main(entry):
        f = main_frame(entry)
        across, along = entry
        arrived(kv_main, f, main_sem)
        if across == 0:
            pass_main(f, up)
            pass_main(f, down)
        if across == -1 and along in PLUS:
            pass_main(f, up)
        if across == 1 and along in MINUS:
            pass_main(f, down)
        share(kv_main, f, main_pair_sem)

    def take_last(entry):
        f = last_frame(entry)
        across, along = entry
        arrived(kv_last, f, last_sem)
        if across == 0:
            pass_last(f, right)
            pass_last(f, left)
        if across == -1 and along in PLUS:
            pass_last(f, right)
        if across == 1 and along in MINUS:
            pass_last(f, left)
        share(kv_last, f, last_pair_sem)

    for dx in (1, 3, 2):
        other = (x + dx) % SIDE
        pltpu.make_async_remote_copy(
            src_ref=q_main.at[other], dst_ref=q_main.at[other], send_sem=send_sem.at[0],
            recv_sem=q_sem.at[other], device_id=pair, device_id_type=MESH,
        ).wait_recv()

    main_frames = [main_frame(entry) for entry in MAIN_ORDER]
    last_frames = [last_frame(entry) for entry in LAST_ORDER]

    def step(k, carry):
        for kk in range(16):
            @pl.when(k == kk)
            def _():
                if kk + 1 < 16:
                    take_last(LAST_ORDER[kk + 1])
                    take_main(MAIN_ORDER[kk + 1])
                arrived_pair(kv_main, main_frames[kk], main_pair_sem)
                arrived_pair(kv_last, last_frames[kk], last_pair_sem)

        f_main, f_last = pick(k, main_frames), pick(k, last_frames)

        def operands(unit):
            if unit < SIDE:
                return q_main[unit], kv_main, f_main, y * SIDE + unit
            return q_ref[:, SIDE * HD:], kv_last, f_last, mine

        def score(unit, s_ref):
            q, kv, f, qf = operands(unit)
            keys = kv[f, :, 0].reshape(2 * tokens, HD)
            s = lax.dot_general(q, keys, (((1,), (1,)), ((), ())), preferred_element_type=jnp.float32)
            s = jnp.where(far[...] <= window[qf, f], s, NEG_FILL)
            old = run_max[unit]
            new = jnp.maximum(old, jnp.max(s, axis=-1, keepdims=True))
            s_ref[...] = s
            run_max[unit] = new
            return new, jnp.exp2((old - new) * scale)

        def gather(unit, s_ref, new, factor):
            q, kv, f, qf = operands(unit)
            weights = jnp.exp2((s_ref[...] - new[:, :1]) * scale)
            part = weights[:, :HD]
            for j in range(1, 2 * tokens // HD):
                part = part + weights[:, HD * j: HD * (j + 1)]
            run_sum[unit] = run_sum[unit] * factor + part
            values = kv[f, :, 1].reshape(2 * tokens, HD)
            run_acc[unit] = run_acc[unit] * factor + jnp.dot(
                weights.astype(jnp.bfloat16), values, preferred_element_type=jnp.float32
            )

        slots = (s_even, s_odd)
        state = score(0, slots[0])
        for unit in range(SIDE + 1):
            following = score(unit + 1, slots[(unit + 1) % 2]) if unit < SIDE else None
            gather(unit, slots[unit % 2], *state)
            state = following
        return carry

    lax.fori_loop(0, 16, step, 0)
    for unit in range(SIDE + 1):
        total = jnp.sum(run_sum[unit], axis=-1, keepdims=True)
        o_ref[unit] = (run_acc[unit] / total).astype(jnp.bfloat16)

    for slot in range(counts["piece"]):
        pltpu.make_async_remote_copy(
            src_ref=kv_main.at[0, 0], dst_ref=kv_main.at[0, 0], send_sem=send_sem.at[slot],
            recv_sem=main_sem.at[0], device_id=pair, device_id_type=MESH,
        ).wait_send()
    for position in range(counts["block"]):
        pltpu.make_async_remote_copy(
            src_ref=q_main.at[0], dst_ref=q_main.at[0], send_sem=send_sem.at[N_SENDS - 1 - position],
            recv_sem=q_sem.at[0], device_id=pair, device_id_type=MESH,
        ).wait_send()


def project_kernel(
    o_ref, w_hbm, out_ref, weights, attended, sent, got, weight_sem, move_sem, o_send, o_recv, z_send, z_recv
):
    tm, z = lax.axis_index("tm"), lax.axis_index("head")
    depth = lax.axis_size("head")
    y, x = tm // SIDE, tm % SIDE
    row = {d: {"tm": y * SIDE + (x + d) % SIDE} for d in (1, 2, 3)}
    ahead, behind = {"head": (z + 1) % depth}, {"head": (z + depth - 1) % depth}
    greet([row[1], row[3], row[2], ahead, behind])

    def head_of(ref, head):
        return ref.at[:, pl.ds(pl.multiple_of(head * HD, HD), HD)]

    returns = [
        pltpu.make_async_remote_copy(
            src_ref=o_ref.at[(x + d) % SIDE], dst_ref=head_of(attended, x), send_sem=o_send.at[d],
            recv_sem=o_recv.at[x], device_id=row[d], device_id_type=MESH,
        )
        for d in (1, 3, 2)
    ]
    for copy in returns:
        copy.start()
    moves = [
        pltpu.make_async_copy(o_ref.at[x], head_of(attended, x), move_sem.at[0]),
        pltpu.make_async_copy(o_ref.at[SIDE], head_of(attended, SIDE), move_sem.at[1]),
    ]
    width = weights.shape[1]
    loads = [
        pltpu.make_async_copy(w_hbm.at[:, pl.ds(c * width, width)], weights.at[c], weight_sem.at[c])
        for c in range(depth)
    ]
    for copy in moves + loads:
        copy.start()
    for copy in moves + loads:
        copy.wait()
    for d in (1, 3, 2):
        other = (x + d) % SIDE
        pltpu.make_async_remote_copy(
            src_ref=o_ref.at[0], dst_ref=head_of(attended, other), send_sem=o_send.at[d],
            recv_sem=o_recv.at[other], device_id=row[d], device_id_type=MESH,
        ).wait_recv()

    half = attended.shape[0] // 2
    longest = depth // 2

    def share(part, owner):
        return jnp.dot(
            attended[part * half: (part + 1) * half, :], weights[owner], preferred_element_type=jnp.float32
        )

    def hop(way, part, t):
        return pltpu.make_async_remote_copy(
            src_ref=sent.at[way, part, t], dst_ref=got.at[way, part, t], send_sem=z_send.at[way, part, t],
            recv_sem=z_recv.at[way, part, t], device_id=(ahead, behind)[way], device_id_type=MESH,
        )

    length = {(0, 0): longest, (1, 1): longest, (0, 1): longest - 1, (1, 0): longest - 1}
    for t in range(longest):
        for way, part in ((0, 0), (1, 1), (0, 1), (1, 0)):
            reach = length[(way, part)] - t
            if reach <= 0:
                continue
            owner = (z + (reach if way == 0 else depth - reach)) % depth
            total = share(part, owner)
            if t:
                hop(way, part, t - 1).wait_recv()
                total = total + got[way, part, t - 1].astype(jnp.float32)
            sent[way, part, t] = total.astype(jnp.bfloat16)
            hop(way, part, t).start()
    for part in range(2):
        total = share(part, z)
        for way in range(2):
            t = length[(way, part)] - 1
            hop(way, part, t).wait_recv()
            total = total + got[way, part, t].astype(jnp.float32)
        out_ref[part * half: (part + 1) * half, :] = total.astype(jnp.bfloat16)
    for copy in returns:
        copy.wait_send()
    for (way, part), steps in length.items():
        for t in range(steps):
            hop(way, part, t).wait_send()


def body(query, key, value, window, out_weight):
    frames_dev, rows_dev, width, feats = query.shape
    tokens = frames_dev * rows_dev * width
    units = feats // HD
    depth = lax.axis_size("head")
    f32, bf16 = jnp.float32, jnp.bfloat16
    vmem, dma = pltpu.VMEM, pltpu.SemaphoreType.DMA
    in_vmem = pl.BlockSpec(memory_space=pltpu.VMEM)
    attended = pl.pallas_call(
        attend_kernel,
        out_shape=jax.ShapeDtypeStruct((units, tokens, HD), bf16),
        in_specs=[pl.BlockSpec(memory_space=pltpu.SMEM)] + [in_vmem] * 3,
        out_specs=in_vmem,
        scratch_shapes=[
            vmem((16, 2, 2, tokens, HD), bf16),
            vmem((16, 2, 2, tokens, HD), bf16),
            vmem((SIDE, tokens, HD), bf16),
            vmem((tokens, 2 * tokens), jnp.int32),
            vmem((tokens, 2 * tokens), f32),
            vmem((tokens, 2 * tokens), f32),
            vmem((units, tokens, HD), f32),
            vmem((units, tokens, HD), f32),
            vmem((units, tokens, HD), f32),
            dma((N_SENDS,)), dma((16,)), dma((16,)), dma((16,)), dma((16,)), dma((SIDE,)), dma((5,)),
        ],
        compiler_params=pltpu.CompilerParams(
            collective_id=0, has_side_effects=True, vmem_limit_bytes=40 * 2**20
        ),
        name="attend",
    )(window, *(a.reshape(tokens, feats) for a in (query, key, value)))
    share = out_weight.shape[1] // depth
    projected = pl.pallas_call(
        project_kernel,
        out_shape=jax.ShapeDtypeStruct((tokens, share), bf16),
        in_specs=[in_vmem, pl.BlockSpec(memory_space=pl.ANY)],
        out_specs=in_vmem,
        scratch_shapes=[
            vmem((depth, feats, share), bf16),
            vmem((tokens, feats), bf16),
            vmem((2, 2, depth // 2, tokens // 2, share), bf16),
            vmem((2, 2, depth // 2, tokens // 2, share), bf16),
            dma((depth,)), dma((2,)), dma((SIDE,)), dma((SIDE,)),
            dma((2, 2, depth // 2)), dma((2, 2, depth // 2)),
        ],
        compiler_params=pltpu.CompilerParams(
            collective_id=1, has_side_effects=True, vmem_limit_bytes=40 * 2**20
        ),
        name="project",
    )(attended, out_weight)
    return projected.reshape(frames_dev, rows_dev, width, share)


def solution(mesh):
    placed = (
        P("tm", "space", None, "head"),
        P("tm", "space", None, "head"),
        P("tm", "space", None, "head"),
        P(),
        P("head", None),
    )
    return jax.shard_map(
        body, mesh=mesh, in_specs=placed, out_specs=P("tm", "space", None, "head"), check_vma=False
    )
```

time: 813 us -> 114 us (0.14)
  waiting for transfers between devices: 288 us -> 0 us
  matrix products: 188 us -> 0 us
  other arithmetic: 145 us -> 0 us
  local copies, waits for them, and re-layouts: 141 us -> 7.31 us
  Pallas kernels: 0 us -> 107 us
  loops' own time: 30.9 us -> 0 us
  between operations: 13.5 us -> 0.03 us
    all_gather x1 -> x0, waiting for transfers between devices: 232 us -> none  [body(): piece = lax.all_gather(padded, 'tm', axis=1, tiled=True)]
    dot_general x33 -> x0, matrix products: 188 us -> none  [the longest x16 91.6 us: absorb(): jnp.einsum('qhd,khd->hqk', queries, keys, preferred_element_type=jnp.floa...]
    pallas_call x0 -> x2, Pallas kernels: none -> 107 us  [the longest x1 61.3 us: body(): pl.pallas_call(attend_kernel, out_shape=jax.ShapeDtypeStruct((units, toke...]
    reduce_sum x16 -> x0, other arithmetic: 78.2 us -> none  [absorb(): new_sum = run_sum * factor + jnp.sum(weights, axis=-1)]
    squeeze x32 -> x0, local copies, waits for them, and re-layouts: 64.9 us -> none  [the longest x16 42.2 us: absorb_frame(): keys = kv_frame[0].reshape(span_rows * width, heads_dev, HD)]
    unnamed x3 -> x0, waiting for transfers between devices: 52.8 us -> none
    another operation x1 -> x0, loops' own time: 30.9 us -> none  [body(): lax.scan(one_frame, empty_state(heads_dev, qcount), jnp.arange(piece.shap...]
    slice x16 -> x0, local copies, waits for them, and re-layouts: 30 us -> none  [absorb_frame(): values = kv_frame[1].reshape(span_rows * width, heads_dev, HD)]
  transfers between devices with their start and end apart: 4 -> 0, of which waited for: 4 -> 0; matrix products, arithmetic and copies ran while one was open for 0% -> 0% of each run, Pallas kernels for 0% -> 0%
where the time goes in v1:
time: 114 us
  Pallas kernels  107 us (94%)
  local copies, waits for them, and re-layouts  7.31 us (6%)
    pallas_call x1, Pallas kernels, body(): pl.pallas_call(attend_kernel, out_shape=jax.ShapeDtypeStruct((units, toke...  61.3 us
    pallas_call x1, Pallas kernels, body(): pl.pallas_call(project_kernel, out_shape=jax.ShapeDtypeStruct((tokens, sh...  45.4 us
    unnamed x11, local copies, waits for them, and re-layouts  7.31 us

profile of v1, /device:TPU:8, one launch (start us, length us, event | category | flops | bytes accessed | tf_op | source)
XLA Modules:
  0.0 114.0 jit_solution(13960898424130556314)
XLA Ops:
  0.0 0.0 copy-start.1
  0.0 1.0 copy-done.1
  1.0 0.0 copy-start.2
  1.0 1.0 copy-done.2
  2.0 0.0 copy-start.3
  2.0 1.0 copy-done.3
  3.0 0.0 copy-start.4
  3.0 0.7 copy-done.4
  3.7 61.3 %attend.1.o_ref = bf16[5,320,128]{2,1,0:T(8,128)(2,1)S(1)} custom-call(s32[16,16]{1,0:T(8,128)S(1)} %copy-done.4, bf16[320,640]{1,0:T(8,128)(2,1)S(1)} %bitcast.5, bf16[320,640]{1,0:T(8,128)(2,1)S(1)} %bitcast.6, bf16[320,640]{1,0:T(8,128)(2,1)S(1)} %bitcast.7), custom_call_target="tpu_custom_call" | custom-call | tf_op jit(solution)/shard_map/attend/pallas_call | solution.py:334
  65.0 0.0 copy-start
  65.0 2.9 %copy-done = bf16[640,5120]{1,0:T(8,128)(2,1)S(1)} copy-done((bf16[640,5120]{1,0:T(8,128)(2,1)S(1)}, bf16[640,5120]{1,0:T(8,128)(2,1)}, u32[]{:S(2)}) %copy-start) | copy-done | bytes 6553624
  67.9 45.4 %project.1 = bf16[320,640]{1,0:T(8,128)(2,1)S(1)} custom-call(bf16[5,320,128]{2,1,0:T(8,128)(2,1)S(1)} %attend.1.o_ref, bf16[640,5120]{1,0:T(8,128)(2,1)S(1)} %copy-done), custom_call_target="tpu_custom_call" | custom-call | tf_op jit(solution)/shard_map/project/pallas_call | solution.py:357
  113.2 0.8 copy.7
Async XLA Ops:
  0.0 1.0 copy-start.1
  1.0 1.0 copy-start.2
  2.0 1.0 copy-start.3
  3.0 0.7 copy-start.4
  65.0 2.9 %copy-start = (bf16[640,5120]{1,0:T(8,128)(2,1)S(1)}, bf16[640,5120]{1,0:T(8,128)(2,1)}, u32[]{:S(2)}) copy-start(bf16[640,5120]{1,0:T(8,128)(2,1)} %w_hbm.1) | copy-start | bytes 19660804

commit v2 on v0

v2 whole, which is shorter than its diff:
```python
import math

import jax
import jax.numpy as jnp
from jax import lax
from jax.experimental import pallas as pl
from jax.experimental.pallas import tpu as pltpu
from jax.sharding import PartitionSpec as P

HD = 128
SIDE = 4
ROW = 80
NEG_FILL = -1e30
MAX_START = -1e20
MESH = pl.DeviceIdType.MESH

GRAY = (0, 1, 3, 2)
PAIRS = (
    ((-1, 0), (1, 0)),
    ((0, 1), (0, 2)),
    ((-1, 1), (1, 1)),
    ((-1, 2), (1, 2)),
    ((0, 3), (2, 0)),
    ((2, 1), (-1, 3)),
    ((1, 3), (2, 2)),
)
FINAL = (2, 3)
EVENTS = {
    ("own", 3): (("main", (-1, 0)), ("main", (1, 0))),
    (0, 2): (("main", (0, 1)), ("main", (0, 2))),
    (1, 3): (("last", 1), ("main", (-1, 1)), ("main", (1, 1))),
    (2, 2): (("last", 3),),
    (2, 3): (("main", (-1, 2)), ("main", (1, 2))),
    (3, 2): (("main", (0, 3)), ("last", 2), ("main", (2, 0))),
    (4, 2): (("main", (2, 1)), ("main", (-1, 3))),
    (5, 2): (("main", (1, 3)), ("main", (2, 2))),
    (6, 2): (("main", (2, 3)),),
}
LAST_AFTER = 3
PLUS = (0, 2)
MINUS = (1, 3)
PIECES, BLOCKS = 56, 24


def pick(index, values):
    out = values[0]
    for position, value in enumerate(values[1:], 1):
        out = jnp.where(index == position, value, out)
    return out


def layer_kernel(
    window_hbm, q_hbm, k_hbm, v_hbm, w_hbm, out_ref,
    window, q_ref, k_ref, v_ref, kv_main, kv_last, q_main, q_last, far, s_even, s_odd,
    run_max, run_sum, run_acc, last_max, last_sum, last_acc, part_sent, part_got,
    o_main, weights, attended, sent, got,
    piece_sem, block_sem, main_sem, main_pair_sem, last_sem, last_pair_sem, q_sem, q_last_sem,
    part_sem, o_sem, local_sem, weight_sem, z_send, z_recv,
):
    scale = math.log2(math.e) / math.sqrt(HD)
    f32, bf16 = jnp.float32, jnp.bfloat16
    tm, core, z = lax.axis_index("tm"), lax.axis_index("space"), lax.axis_index("head")
    depth = lax.axis_size("head")
    y, x = tm // SIDE, tm % SIDE
    tokens = q_hbm.shape[0]
    frame = {
        (dy, dx): ((y + dy) % SIDE) * SIDE + (x + dx) % SIDE for dy in range(4) for dx in range(4)
    }
    column = {d: {"tm": frame[(d, 0)]} for d in (1, 2, 3)}
    row = {d: {"tm": frame[(0, d)]} for d in (1, 2, 3)}
    up, down, right, left = column[1], column[3], row[1], row[3]
    pair = {"space": 1 - core}
    ahead, behind = {"head": (z + 1) % depth}, {"head": (z + depth - 1) % depth}
    mine = frame[(0, 0)]

    def head_of(ref, head):
        return ref.at[:, pl.ds(pl.multiple_of(head * HD, HD), HD)]

    def last_head(ref):
        return ref.at[:, pl.ds(SIDE * HD, HD)]

    width = weights.shape[1]
    first = [
        (q_hbm, q_ref),
        (k_hbm, k_ref),
        (v_hbm, v_ref),
        (head_of(k_hbm, x), kv_main.at[mine, core, 0]),
        (head_of(v_hbm, x), kv_main.at[mine, core, 1]),
        (last_head(k_hbm), kv_last.at[x, core, 0]),
        (last_head(v_hbm), kv_last.at[x, core, 1]),
        (head_of(q_hbm, x), q_main.at[x]),
        (last_head(q_hbm), q_last.at[y]),
        (window_hbm, window),
    ]
    first = [pltpu.make_async_copy(a, b, local_sem.at[i]) for i, (a, b) in enumerate(first)]
    loads = [
        pltpu.make_async_copy(w_hbm.at[:, pl.ds(c * width, width)], weights.at[c], weight_sem.at[c])
        for c in range(depth)
    ]
    for copy in first + loads:
        copy.start()

    barrier = pltpu.get_barrier_semaphore()
    partners = [*column.values(), *row.values(), pair, ahead, behind]
    for partner in partners:
        pl.semaphore_signal(barrier, inc=1, device_id=partner, device_id_type=MESH)
    pl.semaphore_wait(barrier, len(partners))
    for copy in first:
        copy.wait()

    counts = {"piece": 0, "block": 0}

    def send(src, dst, recv_sem, device, kind="piece"):
        sems = piece_sem if kind == "piece" else block_sem
        pltpu.make_async_remote_copy(
            src_ref=src, dst_ref=dst, send_sem=sems.at[counts[kind]], recv_sem=recv_sem,
            device_id=device, device_id_type=MESH,
        ).start()
        counts[kind] += 1

    def arrived(ref, sem):
        pltpu.make_async_remote_copy(
            src_ref=ref, dst_ref=ref, send_sem=piece_sem.at[0], recv_sem=sem,
            device_id=pair, device_id_type=MESH,
        ).wait_recv()

    def pass_main(f, device):
        send(kv_main.at[f, core], kv_main.at[f, core], main_sem.at[f], device)

    def share_main(f):
        send(kv_main.at[f, core], kv_main.at[f, core], main_pair_sem.at[f], pair)

    def share_last(slot):
        send(kv_last.at[slot, core], kv_last.at[slot, core], last_pair_sem.at[slot], pair)

    pass_main(mine, up)
    pass_main(mine, down)
    for d in (1, 3, 2):
        send(head_of(q_ref, (x + d) % SIDE), q_main.at[x], q_sem.at[x], row[d], "block")

    def give(d):
        other = (x + d) % SIDE
        send(head_of(k_ref, other), kv_main.at[mine, core, 0], main_sem.at[mine], row[d], "block")
        send(head_of(v_ref, other), kv_main.at[mine, core, 1], main_sem.at[mine], row[d], "block")

    give(1)
    give(3)
    share_main(mine)
    for d in (1, 3, 2):
        send(q_last.at[y], q_last.at[y], q_last_sem.at[y], column[d], "block")
    send(kv_last.at[x, core], kv_last.at[x, core], last_sem.at[x], right)
    send(kv_last.at[x, core], kv_last.at[x, core], last_sem.at[x], left)
    give(2)
    share_last(x)

    query_row = lax.broadcasted_iota(jnp.int32, (tokens, 2 * tokens), 0) // ROW + core * (tokens // ROW)
    key_row = lax.broadcasted_iota(jnp.int32, (tokens, 2 * tokens), 1) // ROW
    far[...] = jnp.abs(query_row - key_row)
    for ref in (run_max, last_max):
        ref[...] = jnp.full_like(ref, MAX_START)
    for ref in (run_sum, run_acc, last_sum, last_acc):
        ref[...] = jnp.zeros_like(ref)

    def frame_of(entry):
        return frame[(entry[0] % SIDE, GRAY[entry[1]])]

    def take(event):
        kind, entry = event
        if kind == "main":
            f = frame_of(entry)
            across, along = entry
            arrived(kv_main.at[f, core], main_sem.at[f])
            if across == 0:
                pass_main(f, up)
                pass_main(f, down)
            if across == -1 and along in PLUS:
                pass_main(f, up)
            if across == 1 and along in MINUS:
                pass_main(f, down)
            share_main(f)
        else:
            slot = (x + entry) % SIDE
            arrived(kv_last.at[slot, core], last_sem.at[slot])
            if entry == 1:
                half = kv_last.at[slot, core, 1]
                send(half, half, last_sem.at[slot], left, "block")
            if entry == 3:
                half = kv_last.at[slot, core, 0]
                send(half, half, last_sem.at[slot], right, "block")
            share_last(slot)

    def paired(f):
        arrived(kv_main.at[f, 1 - core], main_pair_sem.at[f])

    def job(units, frames, hook):
        span = 2 * tokens

        def score(unit, s_ref):
            q, query_frame, top, _, _ = unit
            best = None
            for n, (kv, f, key_frame) in enumerate(frames):
                keys = kv[f, :, 0].reshape(span, HD)
                s = lax.dot_general(q[...], keys, (((1,), (1,)), ((), ())), preferred_element_type=f32)
                s = jnp.where(far[...] <= window[query_frame, key_frame], s, NEG_FILL)
                s_ref[:, n * span: (n + 1) * span] = s
                for j in range(span // HD):
                    part = s[:, HD * j: HD * (j + 1)]
                    best = part if best is None else jnp.maximum(best, part)
            old = top[...]
            new = jnp.maximum(old, jnp.max(best, axis=-1, keepdims=True))
            top[...] = new
            return new, jnp.exp2((old - new) * scale)

        def gather(unit, s_ref, new, factor):
            _, _, _, total, acc = unit
            all_weights, product = total[...] * factor, acc[...] * factor
            for n, (kv, f, _) in enumerate(frames):
                part = jnp.exp2((s_ref[:, n * span: (n + 1) * span] - new[:, :1]) * scale)
                for j in range(span // HD):
                    all_weights = all_weights + part[:, HD * j: HD * (j + 1)]
                values = kv[f, :, 1].reshape(span, HD)
                product = product + jnp.dot(part.astype(bf16), values, preferred_element_type=f32)
            total[...] = all_weights
            acc[...] = product

        slots = (s_even, s_odd)
        hook(0)
        state = score(units[0], slots[0])
        for n, unit in enumerate(units):
            following = None
            if n + 1 < len(units):
                hook(n + 1)
                following = score(units[n + 1], slots[(n + 1) % 2])
            gather(unit, slots[n % 2], *state)
            state = following

    main_units = [
        (q_main.at[u], y * SIDE + u, run_max.at[u], run_sum.at[u], run_acc.at[u]) for u in range(SIDE)
    ]
    last_units = [
        (q_last.at[u], u * SIDE + x, last_max.at[u], last_sum.at[u], last_acc.at[u]) for u in range(SIDE)
    ]

    def own_hook(unit):
        if unit == 0:
            for d in (1, 3, 2):
                other = (x + d) % SIDE
                arrived(q_main.at[other], q_sem.at[other])
            paired(mine)
        for event in EVENTS.get(("own", unit), ()):
            take(event)

    job(main_units, [(kv_main, mine, mine)], own_hook)

    firsts = [frame_of(a) for a, _ in PAIRS]
    seconds = [frame_of(b) for _, b in PAIRS]

    def step(k, carry):
        def hook(unit):
            for kk in range(len(PAIRS)):
                events = EVENTS.get((kk, unit), ())
                if unit == 0 or events:
                    @pl.when(k == kk)
                    def _():
                        for event in events:
                            take(event)
                        if unit == 0:
                            paired(firsts[kk])
                            paired(seconds[kk])

        one, two = pick(k, firsts), pick(k, seconds)
        job(main_units, [(kv_main, one, one), (kv_main, two, two)], hook)

        @pl.when(k == LAST_AFTER)
        def _():
            for d in (1, 3, 2):
                other = (y + d) % SIDE
                arrived(q_last.at[other], q_last_sem.at[other])
            for d in range(SIDE):
                slot = (x + d) % SIDE
                arrived(kv_last.at[slot, 1 - core], last_pair_sem.at[slot])
            job(last_units, [(kv_last, n, y * SIDE + n) for n in range(SIDE)], lambda unit: None)
            lane = lax.broadcasted_iota(jnp.int32, (tokens, HD), 1)
            for u in range(SIDE):
                total = jnp.sum(last_sum[u], axis=-1, keepdims=True)
                total = jnp.maximum(total, 1e-30)
                part_sent[u, 0] = (last_acc[u] / total).astype(bf16)
                level = last_max[u] * scale + jnp.log2(total)
                high = level.astype(bf16).astype(f32)
                middle = (level - high).astype(bf16).astype(f32)
                low = level - high - middle
                part_sent[u, 1] = jnp.where(lane == 0, high, jnp.where(lane == 1, middle, low)).astype(bf16)
            for d in (1, 3, 2):
                send(part_sent.at[(y + d) % SIDE], part_got.at[y], part_sem.at[y], column[d])
            copy = pltpu.make_async_copy(part_sent.at[y], part_got.at[y], local_sem.at[0])
            copy.start()
            copy.wait()

        return carry

    lax.fori_loop(0, len(PAIRS), step, 0)
    last_one = frame_of(FINAL)

    def final_hook(unit):
        if unit == 0:
            paired(last_one)

    job(main_units, [(kv_main, last_one, last_one)], final_hook)

    for u in range(SIDE):
        total = jnp.sum(run_sum[u], axis=-1, keepdims=True)
        o_main[u] = (run_acc[u] / total).astype(bf16)
    for d in (1, 3, 2):
        send(o_main.at[(x + d) % SIDE], head_of(attended, x), o_sem.at[x], row[d], "block")
    move = pltpu.make_async_copy(o_main.at[x], head_of(attended, x), local_sem.at[0])
    move.start()
    for d in (1, 3, 2):
        other = (y + d) % SIDE
        arrived(part_got.at[other], part_sem.at[other])
    levels = [
        (part_got[u, 1, :, 0:1].astype(f32) + part_got[u, 1, :, 1:2].astype(f32))
        + part_got[u, 1, :, 2:3].astype(f32)
        for u in range(SIDE)
    ]
    highest = jnp.maximum(jnp.maximum(levels[0], levels[1]), jnp.maximum(levels[2], levels[3]))
    shares = [jnp.exp2(level - highest) for level in levels]
    merged = sum(part_got[u, 0].astype(f32) * shares[u] for u in range(SIDE))
    attended[:, SIDE * HD:] = (merged / sum(shares)).astype(bf16)
    move.wait()
    for copy in loads:
        copy.wait()
    for d in (1, 3, 2):
        other = (x + d) % SIDE
        arrived(head_of(attended, other), o_sem.at[other])

    half = tokens // 2
    longest = depth // 2

    def share(part, owner):
        return jnp.dot(
            attended[part * half: (part + 1) * half, :], weights[owner], preferred_element_type=f32
        )

    def hop(way, part, t):
        return pltpu.make_async_remote_copy(
            src_ref=sent.at[way, part, t], dst_ref=got.at[way, part, t], send_sem=z_send.at[way, part, t],
            recv_sem=z_recv.at[way, part, t], device_id=(ahead, behind)[way], device_id_type=MESH,
        )

    length = {(0, 0): longest, (1, 1): longest, (0, 1): longest - 1, (1, 0): longest - 1}
    for t in range(longest):
        for way, part in ((0, 0), (1, 1), (0, 1), (1, 0)):
            reach = length[(way, part)] - t
            if reach <= 0:
                continue
            owner = (z + (reach if way == 0 else depth - reach)) % depth
            total = share(part, owner)
            if t:
                hop(way, part, t - 1).wait_recv()
                total = total + got[way, part, t - 1].astype(f32)
            sent[way, part, t] = total.astype(bf16)
            hop(way, part, t).start()
    for part in range(2):
        total = share(part, z)
        for way in range(2):
            t = length[(way, part)] - 1
            hop(way, part, t).wait_recv()
            total = total + got[way, part, t].astype(f32)
        out_ref[part * half: (part + 1) * half, :] = total.astype(bf16)

    for (way, part), steps in length.items():
        for t in range(steps):
            hop(way, part, t).wait_send()
    for kind, sems, like in (("piece", piece_sem, kv_main.at[0, 0]), ("block", block_sem, q_main.at[0])):
        for slot in range(counts[kind]):
            pltpu.make_async_remote_copy(
                src_ref=like, dst_ref=like, send_sem=sems.at[slot], recv_sem=q_sem.at[0],
                device_id=pair, device_id_type=MESH,
            ).wait_send()


def body(query, key, value, window, out_weight):
    frames_dev, rows_dev, width, feats = query.shape
    tokens = frames_dev * rows_dev * width
    depth = lax.axis_size("head")
    share = out_weight.shape[1] // depth
    f32, bf16 = jnp.float32, jnp.bfloat16
    vmem, dma = pltpu.VMEM, pltpu.SemaphoreType.DMA
    anywhere = pl.BlockSpec(memory_space=pl.ANY)
    projected = pl.pallas_call(
        layer_kernel,
        out_shape=jax.ShapeDtypeStruct((tokens, share), bf16),
        in_specs=[anywhere] * 5,
        out_specs=pl.BlockSpec(memory_space=pltpu.VMEM),
        scratch_shapes=[
            pltpu.SMEM(window.shape, jnp.int32),
            vmem((tokens, feats), bf16), vmem((tokens, feats), bf16), vmem((tokens, feats), bf16),
            vmem((SIDE * SIDE, 2, 2, tokens, HD), bf16),
            vmem((SIDE, 2, 2, tokens, HD), bf16),
            vmem((SIDE, tokens, HD), bf16),
            vmem((SIDE, tokens, HD), bf16),
            vmem((tokens, 2 * tokens), jnp.int32),
            vmem((tokens, SIDE * 2 * tokens), f32),
            vmem((tokens, SIDE * 2 * tokens), f32),
            *[vmem((SIDE, tokens, HD), f32)] * 6,
            vmem((SIDE, 2, tokens, HD), bf16),
            vmem((SIDE, 2, tokens, HD), bf16),
            vmem((SIDE, tokens, HD), bf16),
            vmem((depth, feats, share), bf16),
            vmem((tokens, feats), bf16),
            vmem((2, 2, depth // 2, tokens // 2, share), bf16),
            vmem((2, 2, depth // 2, tokens // 2, share), bf16),
            dma((PIECES,)), dma((BLOCKS,)), dma((16,)), dma((16,)), dma((SIDE,)), dma((SIDE,)),
            dma((SIDE,)), dma((SIDE,)), dma((SIDE,)), dma((SIDE,)), dma((10,)), dma((depth,)),
            dma((2, 2, depth // 2)), dma((2, 2, depth // 2)),
        ],
        compiler_params=pltpu.CompilerParams(
            collective_id=0, has_side_effects=True, vmem_limit_bytes=63 * 2**20
        ),
        name="layer",
    )(window, *(a.reshape(tokens, feats) for a in (query, key, value)), out_weight)
    return projected.reshape(frames_dev, rows_dev, width, share)


def solution(mesh):
    placed = (
        P("tm", "space", None, "head"),
        P("tm", "space", None, "head"),
        P("tm", "space", None, "head"),
        P(),
        P("head", None),
    )
    return jax.shard_map(
        body, mesh=mesh, in_specs=placed, out_specs=P("tm", "space", None, "head"), check_vma=False
    )
```

time: 813 us -> 100 us (0.12)
  waiting for transfers between devices: 288 us -> 0 us
  matrix products: 188 us -> 0 us
  other arithmetic: 145 us -> 0 us
  local copies, waits for them, and re-layouts: 141 us -> 1.79 us
  Pallas kernels: 0 us -> 98.4 us
  loops' own time: 30.9 us -> 0 us
  between operations: 13.5 us -> 0.01 us
    all_gather x1 -> x0, waiting for transfers between devices: 232 us -> none  [body(): piece = lax.all_gather(padded, 'tm', axis=1, tiled=True)]
    dot_general x33 -> x0, matrix products: 188 us -> none  [the longest x16 91.6 us: absorb(): jnp.einsum('qhd,khd->hqk', queries, keys, preferred_element_type=jnp.floa...]
    pallas_call x0 -> x1, Pallas kernels: none -> 98.4 us  [body(): pl.pallas_call(layer_kernel, out_shape=jax.ShapeDtypeStruct((tokens, shar...]
    reduce_sum x16 -> x0, other arithmetic: 78.2 us -> none  [absorb(): new_sum = run_sum * factor + jnp.sum(weights, axis=-1)]
    squeeze x32 -> x0, local copies, waits for them, and re-layouts: 64.9 us -> none  [the longest x16 42.2 us: absorb_frame(): keys = kv_frame[0].reshape(span_rows * width, heads_dev, HD)]
    unnamed x3 -> x0, waiting for transfers between devices: 52.8 us -> none
    another operation x1 -> x0, loops' own time: 30.9 us -> none  [body(): lax.scan(one_frame, empty_state(heads_dev, qcount), jnp.arange(piece.shap...]
    slice x16 -> x0, local copies, waits for them, and re-layouts: 30 us -> none  [absorb_frame(): values = kv_frame[1].reshape(span_rows * width, heads_dev, HD)]
  transfers between devices with their start and end apart: 4 -> 0, of which waited for: 4 -> 0; matrix products, arithmetic and copies ran while one was open for 0% -> 0% of each run, Pallas kernels for 0% -> 0%
where the time goes in v2:
time: 100 us
  Pallas kernels  98.4 us (98%)
  local copies, waits for them, and re-layouts  1.79 us (2%)
    pallas_call x1, Pallas kernels, body(): pl.pallas_call(layer_kernel, out_shape=jax.ShapeDtypeStruct((tokens, shar...  98.4 us

profile of v2, /device:TPU:8, one launch (start us, length us, event | category | flops | bytes accessed | tf_op | source)
XLA Modules:
  0.0 100.2 jit_solution(5462695506120075782)
XLA Ops:
  0.0 98.4 %layer.1 = bf16[320,640]{1,0:T(8,128)(2,1)} custom-call(s32[16,16]{1,0:T(8,128)} %window_hbm.1, bf16[320,640]{1,0:T(8,128)(2,1)} %bitcast.5, bf16[320,640]{1,0:T(8,128)(2,1)} %bitcast.6, bf16[320,640]{1,0:T(8,128)(2,1)} %bitcast.7, bf16[640,5120]{1,0:T(8,128)(2,1)} %w_hbm.1), custom_call_target="tpu_custom_call" | custom-call | tf_op jit(solution)/shard_map/layer/pallas_call | solution.py:390
  98.4 1.8 %copy.7 = bf16[1,4,80,640]{3,2,1,0:T(8,128)(2,1)} copy(bf16[1,4,80,640]{3,2,1,0:T(8,128)(2,1)} %bitcast.4) | data formatting | bytes 819200
